TPU v7x, 256 devices: a whole 4x4x8 slice. The times are simulated.
256 devices in a mesh: bank: 64 (over x_hi, z, y), tp: 4 (over x_lo, core).
Axes of the slice: x: 4 (x_hi: 2, x_lo: 2; x = x_hi * 2 + x_lo), y: 4, z: 8, core: 2. Of those that a mesh axis runs over, the one named last changes fastest.
Arguments:
- hidden: bfloat16 [128, 512, 14336], P('bank', None, 'tp'), may hold values from -6 to 6
- out_grad: bfloat16 [128, 512, 4096], P('bank', None, 'tp'), may hold values from -6 to 6
- proj_in: bfloat16 [64, 14336], P(None, 'tp'), may hold values from -0.046875 to 0.046875
- proj_out: bfloat16 [64, 4096], P(None, 'tp'), may hold values from -0.09375 to 0.09375
- lengths: int32 [128], P('bank'), may hold values from 1 to 512, 49152 in all
- pair_perm: int32 [128], replicated, may hold values from 0 to 127, each once
- bank_slab: bfloat16 [65536, 4096], P('bank', 'tp'), may hold values from -6 to 6
Outputs:
- scores: float32 [64, 65536], P('tp', 'bank')
Inputs may be any that keep to these rules, and one draw needn't show every extreme that they name: pair_perm holds every variant index exactly once. `lengths`: some prompt fills all 512 slots.
All inputs are finite; a program needn't handle non-finite values. No bound on the sum of `lengths` on one device may be relied on, other than what follows from the above.
Results may differ from a plain program's by a relative error of at most 0.0029.
Values sent between devices are 32-bit elements; how exact they have to be, the bound alone decides.
A program may use at most 64 MiB of HBM per device.

v0:
```python
import jax
import jax.numpy as jnp
from jax import lax
from jax.sharding import PartitionSpec as P

epsilon = 1e-06


def per_device(hidden, out_grad, proj_in, proj_out, lengths, pair_perm, bank_slab):
    ex_dev, seq_len, ff_dev = hidden.shape
    factor_rank = proj_in.shape[0]
    tp_count = lax.axis_size("tp")
    share_rows = factor_rank // tp_count
    tok_rows = hidden.reshape(ex_dev * seq_len, ff_dev)
    grad_rows = out_grad.reshape(ex_dev * seq_len, out_grad.shape[2])
    in_part = jnp.einsum("rf,tf->rt", proj_in, tok_rows, preferred_element_type=jnp.float32)
    out_part = jnp.einsum("rd,td->rt", proj_out, grad_rows, preferred_element_type=jnp.float32)
    in_all, out_all = lax.psum((in_part, out_part), "tp")
    in_mine = lax.dynamic_slice_in_dim(in_all, lax.axis_index("tp") * share_rows, share_rows, 0)
    positions = jnp.arange(seq_len, dtype=jnp.int32)
    live_mask = (positions[None, :] < lengths[:, None]).astype(jnp.float32)
    in_three = in_mine.reshape(share_rows, ex_dev, seq_len) * live_mask[None, :, :]
    out_three = out_all.reshape(factor_rank, ex_dev, seq_len)
    grads = jnp.einsum("ies,jes->eij", in_three, out_three, precision=lax.Precision.HIGHEST)
    grads = grads.reshape(ex_dev, share_rows * factor_rank)
    benign = pair_perm[0::2]
    harmful = pair_perm[1::2]
    all_grads = lax.all_gather(grads, "bank", axis=0, tiled=True)
    example_ids = jnp.arange(all_grads.shape[0], dtype=jnp.int32)
    pair_signs = (example_ids[None, :] == harmful[:, None]).astype(jnp.float32) - (
        example_ids[None, :] == benign[:, None]
    ).astype(jnp.float32)
    queries = jnp.dot(pair_signs, all_grads, precision=lax.Precision.HIGHEST)
    query_part = jnp.sum(queries * queries, axis=1)
    slab_wide = bank_slab.astype(jnp.float32)
    bank_part = jnp.sum(slab_wide * slab_wide, axis=1)
    query_sq, bank_sq = lax.psum((query_part, bank_part), "tp")
    query_low = queries.astype(jnp.bfloat16)
    pair_count = queries.shape[0]
    pairs_mine = pair_count // tp_count
    dots = lax.psum_scatter(
        lax.dot_general(
            query_low, bank_slab, (((1,), (1,)), ((), ())), preferred_element_type=jnp.float32
        ),
        "tp",
        scatter_dimension=0,
        tiled=True,
    )
    query_mine = lax.dynamic_slice_in_dim(
        query_sq, lax.axis_index("tp") * pairs_mine, pairs_mine, 0
    )
    return (
        dots
        * factor_rank
        * lax.rsqrt(query_mine + epsilon)[:, None]
        * lax.rsqrt(bank_sq + epsilon)[None, :]
    )


def solution(mesh):
    return jax.shard_map(
        per_device,
        mesh=mesh,
        in_specs=(
            P("bank", None, "tp"),
            P("bank", None, "tp"),
            P(None, "tp"),
            P(None, "tp"),
            P("bank"),
            P(),
            P("bank", "tp"),
        ),
        out_specs=P("tp", "bank"),
        check_vma=False,
    )
```

profile of v0, /device:TPU:1, one launch (start us, length us, event | category | flops | bytes accessed | tf_op | source)
XLA Modules:
  0.0 274.3 jit_solution(10950495381931768916)
XLA Ops:
  6.5 0.0 copy-start
  6.5 0.0 copy-start.1
  6.5 0.0 all-reduce.4.cloned.1.call-start
  6.5 1.6 copy-done
  8.1 1.7 fusion.11
  9.8 0.7 copy.17
  10.5 0.0 copy-done.1
  10.5 0.0 copy-start.3
  10.5 0.0 copy-start.2
  10.5 6.1 %fusion.10 = f32[64,1024]{1,0:T(8,128)} fusion(bf16[64,3584]{1,0:T(8,128)(2,1)S(1)} %copy-done.1, bf16[1024,3584]{1,0:T(8,128)(2,1)} %bitcast.18), kind=kOutput, calls=%fused_computation.21 | convolution fusion | flops 469762048 | bytes 8060928 | tf_op jit(solution)/shard_map/rf,tf->rt/dot_general | solution.py:16
  16.6 0.0 all-reduce.4.cloned.1.call-update
  16.7 0.0 reduce-scatter.2.cloned.1.call-start
  16.7 0.0 copy-done.3
  16.7 0.2 slice.7
  16.9 0.2 slice.6
  17.1 0.0 copy-done.2
  17.1 0.1 compare_convert_fusion
  17.1 46.7 %all-reduce.4.cloned.1.call-done = (f32[64,2,512]{2,0,1:T(8,128)}, f32[64,1024]{1,0:T(8,128)}) async-done(((f32[64,2,512]{2,0,1:T(8,128)}, f32[64,1024]{1,0:T(8,128)}), (f32[64,2,512]{2,0,1:T(8,128)}, f32[64,1024]{1,0:T(8,128)})) %all-reduce.4.cloned.1.call-update) | async-done | bytes 524304 | tf_op jit(solution)/shard_map/psum | solution.py:18
  63.9 0.8 constant_dynamic-slice_fusion
  64.7 0.1 reshape.39
  64.8 1.3 fusion.2
  66.1 0.1 reshape.43
  66.2 156.8 %all-gather = f32[64,2,1024]{2,1,0:T(2,128)S(1)} all-gather(f32[1,2,1024]{2,1,0:T(2,128)S(1)} %reshape.43), channel_id=1, replica_groups=mesh['bank'=64,'tp'=4] {'bank'}, dimensions={0}, use_global_device_ids=true | all-gather | bytes 532480 | tf_op jit(solution)/shard_map/all_gather | solution.py:28
  223.0 0.4 reshape.44
  223.3 0.5 multiply_reduce_fusion.1
  223.9 3.0 %fusion = f32[64,1024]{1,0:T(8,128)} fusion(bf16[1024,1024]{1,0:T(8,128)(2,1)} %param.13, bf16[64,1024]{1,0:T(8,128)(2,1)S(1)} %get-tuple-element.10), kind=kOutput, calls=%fused_computation.3 | convolution fusion | flops 134217728 | bytes 2490368 | tf_op jit(solution)/shard_map/dot_general | solution.py:42
  226.9 0.0 reduce-scatter.2.cloned.1.call-update
  226.9 2.1 multiply_reduce_fusion
  229.0 32.7 %all-reduce = (f32[1024]{0:T(1024)S(1)}, f32[64]{0:T(128)S(1)}) all-reduce(f32[1024]{0:T(1024)S(1)} %multiply_reduce_fusion, f32[64]{0:T(128)S(1)} %get-tuple-element.9), channel_id=1, replica_groups=mesh['bank'=64,'tp'=4] {'tp'}, use_global_device_ids=true, to_apply=%region_6.0 | all-reduce | flops 1088 | bytes 8704 | tf_op jit(solution)/shard_map/psum | solution.py:37
  261.7 0.1 rsqrt_multiply_fusion
  261.8 4.1 %reduce-scatter.2.cloned.1.call-done = f32[16,1024]{1,0:T(8,128)} async-done(((f32[64,1024]{1,0:T(8,128)}), f32[16,1024]{1,0:T(8,128)}) %reduce-scatter.2.cloned.1.call-update) | async-done | bytes 65552 | tf_op jit(solution)/shard_map/reduce_scatter | solution.py:41
  265.9 1.5 multiply_multiply_fusion
  (3 shorter events, 0.0 us)
Async XLA Ops:
  6.5 1.6 copy-start
  6.5 4.0 %copy-start.1 = (bf16[64,3584]{1,0:T(8,128)(2,1)S(1)}, bf16[64,3584]{1,0:T(8,128)(2,1)}, u32[]{:S(2)}) copy-start(bf16[64,3584]{1,0:T(8,128)(2,1)} %param.9) | copy-start | bytes 1376260
  6.5 57.3 %all-reduce.4.cloned.1.call-start = ((), (), s32[]{:S(2)}) async-start(), calls=%async_computation.2 | async-start | bytes 1048576 | tf_op jit(solution)/shard_map/psum | solution.py:18
  10.5 6.2 %copy-start.3 = (s32[128]{0:T(128)S(1)}, s32[128]{0:T(128)}, u32[]{:S(2)}) copy-start(s32[128]{0:T(128)} %param.12) | copy-start | bytes 1540
  10.5 6.5 %copy-start.2 = (s32[2]{0:T(128)S(1)}, s32[2]{0:T(128)}, u32[]{:S(2)}) copy-start(s32[2]{0:T(128)} %param.11) | copy-start | bytes 28
  16.7 249.2 %reduce-scatter.2.cloned.1.call-start = ((), (), s32[]{:S(2)}) async-start(), calls=%async_computation.1 | async-start | bytes 327680 | tf_op jit(solution)/shard_map/reduce_scatter | solution.py:41
Sparse Core Ops, SparseCore 0:
  16.8 47.0 all-reduce.3
  227.1 38.8 reduce-scatter.1
where the time goes:
time: 275 us; the launch traced here: 274 us
  blocking collectives  190 us (69%)
  waiting for transfers between devices  50.9 us (19%)
  between operations  13.5 us (5%)
  matrix products  12.6 us (5%)
  local copies, waits for them, and re-layouts  3.99 us (1%)
  other arithmetic  3.78 us (1%)
    all_gather x1, blocking collectives, per_device(): all_grads = lax.all_gather(grads, 'bank', axis=0, tiled=True)  157 us
    psum x1, waiting for transfers between devices, per_device(): in_all, out_all = lax.psum((in_part, out_part), 'tp')  46.7 us
    psum x1, blocking collectives, per_device(): query_sq, bank_sq = lax.psum((query_part, bank_part), 'tp')  32.7 us
    dot_general x1, matrix products, per_device(): jnp.einsum('rf,tf->rt', proj_in, tok_rows, preferred_element_type=jnp.flo...  6.13 us
  transfers between devices with their start and end apart: 2, of which 2 were waited for; matrix products, arithmetic and copies ran while one was open for 1% of the time, Pallas kernels for 0%

commit v1 on v0

--- a/solution.py
+++ b/solution.py
@@ -25,7 +25,10 @@
     grads = grads.reshape(ex_dev, share_rows * factor_rank)
     benign = pair_perm[0::2]
     harmful = pair_perm[1::2]
-    all_grads = lax.all_gather(grads, "bank", axis=0, tiled=True)
+    size = lax.axis_size("bank")
+    shards = jnp.stack([grads for _ in range(size)])
+    shards = lax.all_to_all(shards, "bank", split_axis=0, concat_axis=0)
+    all_grads = jnp.concatenate(shards, axis=0)
     example_ids = jnp.arange(all_grads.shape[0], dtype=jnp.int32)
     pair_signs = (example_ids[None, :] == harmful[:, None]).astype(jnp.float32) - (
         example_ids[None, :] == benign[:, None]

time: 275 us -> 127 us (0.46)
  blocking collectives: 190 us -> 7.37 us
  waiting for transfers between devices: 50.9 us -> 71.6 us
  starting transfers between devices: 0.04 us -> 12.4 us
    all_gather x1 -> x0, blocking collectives: 157 us -> none  [per_device(): all_grads = lax.all_gather(grads, 'bank', axis=0, tiled=True)]
    psum x1, blocking collectives: 32.7 us -> 7.37 us  [per_device(): query_sq, bank_sq = lax.psum((query_part, bank_part), 'tp')]
    all_to_all x0 -> x1, waiting for transfers between devices: none -> 17.5 us  [per_device(): shards = lax.all_to_all(shards, 'bank', split_axis=0, concat_axis=0)]
    all_to_all x0 -> x1, starting transfers between devices: none -> 12.3 us  [per_device(): shards = lax.all_to_all(shards, 'bank', split_axis=0, concat_axis=0)]
    reduce_scatter x1, waiting for transfers between devices: 4.13 us -> 6.93 us  [per_device(): lax.psum_scatter(lax.dot_general(query_low, bank_slab, (((1,), (1,)), (()...]
  transfers between devices with their start and end apart: 2 -> 3, of which waited for: 2 -> 3; matrix products, arithmetic and copies ran while one was open for 1% -> 2% of each run, Pallas kernels for 0% -> 0%
where the time goes in v1:
time: 127 us; the launch traced here: 126 us
  waiting for transfers between devices  71.6 us (56%)
  between operations  13.5 us (11%)
  matrix products  12.6 us (10%)
  starting transfers between devices  12.4 us (10%)
  blocking collectives  7.37 us (6%)
  local copies, waits for them, and re-layouts  4.9 us (4%)
  other arithmetic  3.78 us (3%)
    psum x1, waiting for transfers between devices, per_device(): in_all, out_all = lax.psum((in_part, out_part), 'tp')  47.2 us
    all_to_all x1, waiting for transfers between devices, per_device(): shards = lax.all_to_all(shards, 'bank', split_axis=0, concat_axis=0)  17.5 us
    all_to_all x1, starting transfers between devices, per_device(): shards = lax.all_to_all(shards, 'bank', split_axis=0, concat_axis=0)  12.3 us
    psum x1, blocking collectives, per_device(): query_sq, bank_sq = lax.psum((query_part, bank_part), 'tp')  7.37 us
    reduce_scatter x1, waiting for transfers between devices, per_device(): lax.psum_scatter(lax.dot_general(query_low, bank_slab, (((1,), (1,)), (()...  6.93 us
    dot_general x1, matrix products, per_device(): jnp.einsum('rf,tf->rt', proj_in, tok_rows, preferred_element_type=jnp.flo...  6.12 us
    dot_general x1, matrix products, per_device(): lax.dot_general(query_low, bank_slab, (((1,), (1,)), ((), ())), preferred...  3.05 us
  transfers between devices with their start and end apart: 3, of which 3 were waited for; matrix products, arithmetic and copies ran while one was open for 2% of the time, Pallas kernels for 0%

profile of v1, /device:TPU:1, one launch (start us, length us, event | category | flops | bytes accessed | tf_op | source)
XLA Modules:
  0.0 126.1 jit_solution(10100173716899101007)
XLA Ops:
  6.5 0.0 copy-start
  6.5 0.0 copy-start.1
  6.5 0.0 all-reduce.4.cloned.1.call-start
  6.5 1.6 %copy-done = bf16[2,512,1024]{2,1,0:T(8,128)(2,1)S(1)} copy-done((bf16[2,512,1024]{2,1,0:T(8,128)(2,1)S(1)}, bf16[2,512,1024]{2,1,0:T(8,128)(2,1)}, u32[]{:S(2)}) %copy-start) | copy-done | bytes 2097176
  8.1 1.7 %fusion.11 = f32[64,1024]{1,0:T(8,128)S(1)} fusion(bf16[64,1024]{1,0:T(8,128)(2,1)} %param.10, bf16[1024,1024]{1,0:T(8,128)(2,1)S(1)} %bitcast.17), kind=kOutput, calls=%fused_computation.22 | convolution fusion | flops 134217728 | bytes 2490368 | tf_op jit(solution)/shard_map/rd,td->rt/dot_general | solution.py:17
  9.8 0.7 copy.15
  10.5 0.0 copy-done.1
  10.5 0.0 copy-start.2
  10.5 6.1 %fusion.10 = f32[64,1024]{1,0:T(8,128)} fusion(bf16[64,3584]{1,0:T(8,128)(2,1)S(1)} %copy-done.1, bf16[1024,3584]{1,0:T(8,128)(2,1)} %bitcast.18), kind=kOutput, calls=%fused_computation.21 | convolution fusion | flops 469762048 | bytes 8060928 | tf_op jit(solution)/shard_map/rf,tf->rt/dot_general | solution.py:16
  16.6 0.0 copy-start.3
  16.6 0.0 all-reduce.4.cloned.1.call-update
  16.6 0.0 copy-done.2
  16.7 0.1 compare_convert_fusion
  16.7 47.2 %all-reduce.4.cloned.1.call-done = (f32[64,2,512]{2,0,1:T(8,128)}, f32[64,1024]{1,0:T(8,128)}) async-done(((f32[64,2,512]{2,0,1:T(8,128)}, f32[64,1024]{1,0:T(8,128)}), (f32[64,2,512]{2,0,1:T(8,128)}, f32[64,1024]{1,0:T(8,128)})) %all-reduce.4.cloned.1.call-update) | async-done | bytes 524304 | tf_op jit(solution)/shard_map/psum | solution.py:18
  63.9 0.8 constant_dynamic-slice_fusion
  64.8 0.1 reshape.41
  64.8 1.3 %fusion.2 = f32[2,16,64]{2,1,0:T(8,128)S(1)} fusion(f32[64,2,512]{2,0,1:T(8,128)} %get-tuple-element.7, f32[16,2,512]{2,1,0:T(2,128)S(1)} %bitcast.22), kind=kOutput, calls=%fused_computation.5 | convolution fusion | flops 12582912 | bytes 335872 | tf_op jit(solution)/shard_map/ies,jes->eij/dot_general | solution.py:24
  66.1 0.1 stack_reshape.2
  66.2 0.9 stack.3
  67.1 12.3 %all-to-all-start = ((f32[64,2,1024]{2,1,0:T(2,128)}), f32[64,2,1024]{2,1,0:T(2,128)S(1)}, u32[]{:S(2)}, u32[]{:S(2)}) async-start(f32[64,2,1024]{2,1,0:T(2,128)} %stack.3), calls=%async_computation | async-start | bytes 1048576 | tf_op jit(solution)/shard_map/all_to_all | solution.py:30
  79.4 0.0 reduce-scatter.2.cloned.1.call-start
  79.5 0.0 copy-done.3
  79.5 0.2 slice.6
  79.7 0.2 slice.7
  79.8 17.5 %all-to-all-done = f32[64,2,1024]{2,1,0:T(2,128)S(1)} async-done(((f32[64,2,1024]{2,1,0:T(2,128)}), f32[64,2,1024]{2,1,0:T(2,128)S(1)}, u32[]{:S(2)}, u32[]{:S(2)}) %all-to-all-start) | async-done | bytes 524320 | tf_op jit(solution)/shard_map/all_to_all | solution.py:30
  97.3 0.4 reshape.44
  97.7 0.5 multiply_reduce_fusion.1
  98.2 3.0 %fusion = f32[64,1024]{1,0:T(8,128)} fusion(bf16[1024,1024]{1,0:T(8,128)(2,1)} %param.13, bf16[64,1024]{1,0:T(8,128)(2,1)S(1)} %get-tuple-element.10), kind=kOutput, calls=%fused_computation.3 | convolution fusion | flops 134217728 | bytes 2490368 | tf_op jit(solution)/shard_map/dot_general | solution.py:45
  101.2 0.0 reduce-scatter.2.cloned.1.call-update
  101.3 2.1 %multiply_reduce_fusion = f32[1024]{0:T(1024)S(1)} fusion(bf16[1024,1024]{1,0:T(8,128)(2,1)} %param.13), kind=kLoop, calls=%fused_computation | loop fusion | flops 3144704 | bytes 2101248 | tf_op jit(solution)/shard_map/reduce_sum | solution.py:39
  103.3 7.4 %all-reduce = (f32[1024]{0:T(1024)S(1)}, f32[64]{0:T(128)S(1)}) all-reduce(f32[1024]{0:T(1024)S(1)} %multiply_reduce_fusion, f32[64]{0:T(128)S(1)} %get-tuple-element.9), channel_id=1, replica_groups=mesh['bank'=64,'tp'=4] {'tp'}, use_global_device_ids=true, to_apply=%region_6.0 | all-reduce | flops 1088 | bytes 8704 | tf_op jit(solution)/shard_map/psum | solution.py:40
  110.7 0.1 rsqrt_multiply_fusion
  110.8 6.9 %reduce-scatter.2.cloned.1.call-done = f32[16,1024]{1,0:T(8,128)} async-done(((f32[64,1024]{1,0:T(8,128)}), f32[16,1024]{1,0:T(8,128)}) %reduce-scatter.2.cloned.1.call-update) | async-done | bytes 65552 | tf_op jit(solution)/shard_map/reduce_scatter | solution.py:44
  117.7 1.5 %multiply_multiply_fusion = f32[16,1024]{1,0:T(8,128)} fusion(f32[16,1024]{1,0:T(8,128)} %reduce-scatter.2.cloned.1.call-done, f32[1024]{0:T(1024)S(1)} %add_rsqrt_fusion, f32[16]{0:T(128)S(1)} %rsqrt_multiply_fusion), kind=kLoop, calls=%fused_computation.7 | loop fusion | flops 32768 | bytes 135232 | tf_op jit(solution)/shard_map/mul | solution.py:56
  (3 shorter events, 0.0 us)
Async XLA Ops:
  6.5 1.6 %copy-start = (bf16[2,512,1024]{2,1,0:T(8,128)(2,1)S(1)}, bf16[2,512,1024]{2,1,0:T(8,128)(2,1)}, u32[]{:S(2)}) copy-start(bf16[2,512,1024]{2,1,0:T(8,128)(2,1)} %param.8) | copy-start | bytes 6291460
  6.5 4.0 %copy-start.1 = (bf16[64,3584]{1,0:T(8,128)(2,1)S(1)}, bf16[64,3584]{1,0:T(8,128)(2,1)}, u32[]{:S(2)}) copy-start(bf16[64,3584]{1,0:T(8,128)(2,1)} %param.9) | copy-start | bytes 1376260
  6.5 57.4 %all-reduce.4.cloned.1.call-start = ((), (), s32[]{:S(2)}) async-start(), calls=%async_computation.3 | async-start | bytes 1048576 | tf_op jit(solution)/shard_map/psum | solution.py:18
  10.5 6.2 %copy-start.2 = (s32[2]{0:T(128)S(1)}, s32[2]{0:T(128)}, u32[]{:S(2)}) copy-start(s32[2]{0:T(128)} %param.11) | copy-start | bytes 28
  16.6 62.9 %copy-start.3 = (s32[128]{0:T(128)S(1)}, s32[128]{0:T(128)}, u32[]{:S(2)}) copy-start(s32[128]{0:T(128)} %param.12) | copy-start | bytes 1540
  67.1 30.2 %all-to-all-start = ((f32[64,2,1024]{2,1,0:T(2,128)}), f32[64,2,1024]{2,1,0:T(2,128)S(1)}, u32[]{:S(2)}, u32[]{:S(2)}) async-start(f32[64,2,1024]{2,1,0:T(2,128)} %stack.3), calls=%async_computation | async-start | bytes 1048576 | tf_op jit(solution)/shard_map/all_to_all | solution.py:30
  79.4 38.3 %reduce-scatter.2.cloned.1.call-start = ((), (), s32[]{:S(2)}) async-start(), calls=%async_computation.2 | async-start | bytes 327680 | tf_op jit(solution)/shard_map/reduce_scatter | solution.py:44
Sparse Core Ops, SparseCore 0:
  16.8 47.0 all-reduce.3
  101.4 16.3 reduce-scatter.1
